TPU v7x, 32 devices: a whole 2x2x4 slice. The times are simulated.
32 devices in a mesh: dp: 16 (over z, x, core), tensor: 2 (over y).
Axes of the slice: x: 2, y: 2, z: 4, core: 2. Of those that a mesh axis runs over, the one named last changes fastest.
Arguments:
- inputs: bfloat16 [6272, 512], P('dp'), may hold values from -6 to 6
- ln1_gain: float32 [512], replicated, may hold values from 0.5 to 1.5
- ln1_shift: float32 [512], replicated, may hold values from -3 to 3
- w_qkv: bfloat16 [512, 3, 512], P(None, None, 'tensor'), may hold values from -0.25 to 0.25
- qv_bias: float32 [2, 512], P(None, 'tensor'), may hold values from -3 to 3
- bias_table: float32 [169, 16], P(None, 'tensor'), may hold values from -6 to 320
- rel_index: int32 [49, 49], replicated, may hold values from 0 to 168
- regions: int32 [196], replicated, may hold values from 0 to 8
- w_proj: bfloat16 [512, 512], P('tensor'), may hold values from -0.5 to 0.5
- proj_bias: float32 [512], replicated, may hold values from -3 to 3
- ln2_gain: float32 [512], replicated, may hold values from 0.5 to 1.5
- ln2_shift: float32 [512], replicated, may hold values from -3 to 3
- w_fc1: bfloat16 [512, 2048], P(None, 'tensor'), may hold values from -0.25 to 0.25
- fc1_bias: float32 [2048], P('tensor'), may hold values from -3 to 3
- w_fc2: bfloat16 [2048, 512], P('tensor'), may hold values from -0.1875 to 0.1875
- fc2_bias: float32 [512], replicated, may hold values from -3 to 3
- grad_output: bfloat16 [6272, 512], P('dp'), may hold values from -12 to 12
Outputs:
- output: bfloat16 [6272, 512], P('dp')
- grad_input: float32 [6272, 512], P('dp')
- grad_ln1_gain: float32 [512], replicated
- grad_ln1_shift: float32 [512], replicated
- grad_qkv: float32 [512, 3, 512], P(None, None, 'tensor')
- grad_qv_bias: float32 [2, 512], P(None, 'tensor')
- grad_table: float32 [169, 16], P(None, 'tensor')
- grad_proj: float32 [512, 512], P('tensor')
- grad_proj_bias: float32 [512], replicated
- grad_ln2_gain: float32 [512], replicated
- grad_ln2_shift: float32 [512], replicated
- grad_fc1: float32 [512, 2048], P(None, 'tensor')
- grad_fc1_bias: float32 [2048], P('tensor')
- grad_fc2: float32 [2048, 512], P('tensor')
- grad_fc2_bias: float32 [512], replicated
All inputs are finite; a program needn't handle non-finite values.
Results may differ from a plain program's by a relative error of at most 0.017.
Values may be sent and summed in bfloat16 or wider, within the bound.
No kernel may reach another device: no remote copies, remote signals or barrier semaphores. Data moves between devices by JAX's collectives and lax.ppermute only.
A program may use at most 64 MiB of HBM per device.

v0:
```python
import jax
import jax.numpy as jnp
from jax import lax
from jax.sharding import PartitionSpec as P

HEAD_DIM = 32
SIDE = 14
WIN = 7
SHIFT = 3
NORM_EPS = 1e-05
MASKED = -1e30


def layer_norm(values, norm_gain, norm_shift):
    centered = values - jnp.mean(values, axis=-1, keepdims=True)
    inverse = lax.rsqrt(jnp.mean(centered * centered, axis=-1, keepdims=True) + NORM_EPS)
    normed = centered * inverse
    return (normed * norm_gain + norm_shift, normed, inverse)


def norm_backward(upstream, normed, inverse, norm_gain):
    weighted = upstream * norm_gain
    return inverse * (
        weighted
        - jnp.mean(weighted, axis=-1, keepdims=True)
        - normed * jnp.mean(weighted * normed, axis=-1, keepdims=True)
    )


def gelu_exact(hidden):
    return 0.5 * hidden * (1.0 + jax.scipy.special.erf(hidden * 0.7071067811865476))


def gelu_slope(hidden):
    return (
        0.5 * (1.0 + jax.scipy.special.erf(hidden * 0.7071067811865476))
        + hidden * jnp.exp(-0.5 * hidden * hidden) * 0.3989422804014327
    )


def to_windows(tensor, images):
    heads_here = tensor.shape[1]
    head_depth = tensor.shape[2]
    across = SIDE // WIN
    layout = tensor.reshape(images, SIDE, SIDE, heads_here, head_depth)
    layout = jnp.roll(layout, (-SHIFT, -SHIFT), axis=(1, 2))
    layout = layout.reshape(images, across, WIN, across, WIN, heads_here, head_depth).transpose(
        0, 1, 3, 5, 2, 4, 6
    )
    return layout.reshape(images * across * across, heads_here, WIN * WIN, head_depth)


def from_windows(tensor, images):
    heads_here = tensor.shape[1]
    head_depth = tensor.shape[3]
    across = SIDE // WIN
    layout = tensor.reshape(images, across, across, heads_here, WIN, WIN, head_depth).transpose(
        0, 1, 4, 2, 5, 3, 6
    )
    layout = jnp.roll(
        layout.reshape(images, SIDE, SIDE, heads_here, head_depth), (SHIFT, SHIFT), axis=(1, 2)
    )
    return layout.reshape(images * SIDE * SIDE, heads_here * head_depth)


def window_scores(queries, keys_win, rel_bias, allowed, images):
    raw_scores = jnp.einsum(
        "whie,whje->whij", queries, keys_win, preferred_element_type=jnp.float32
    )
    layout = (
        raw_scores.reshape((images, allowed.shape[0]) + raw_scores.shape[1:]) + rel_bias[None, None]
    )
    return jnp.where(allowed[None, :, None], layout, MASKED)


def local(
    inputs,
    ln1_gain,
    ln1_shift,
    w_qkv,
    qv_bias,
    bias_table,
    rel_index,
    regions,
    w_proj,
    proj_bias,
    ln2_gain,
    ln2_shift,
    w_fc1,
    fc1_bias,
    w_fc2,
    fc2_bias,
    grad_output,
):
    tokens_here = inputs.shape[0]
    width = inputs.shape[1]
    images = tokens_here // (SIDE * SIDE)
    inner = w_qkv.shape[2]
    heads_here = inner // HEAD_DIM
    q_factor = HEAD_DIM ** (-0.5)
    across = SIDE // WIN
    positions = WIN * WIN
    residual_in = inputs.astype(jnp.float32)
    normed_one, unit_one, inverse_one = layer_norm(residual_in, ln1_gain, ln1_shift)
    normed_one_b = normed_one.astype(jnp.bfloat16)
    qkv_weight = w_qkv.reshape(width, 3 * inner)
    projected = jnp.dot(normed_one_b, qkv_weight, preferred_element_type=jnp.float32).reshape(
        tokens_here, 3, inner
    )
    queries = ((projected[:, 0] + qv_bias[0]) * q_factor).astype(jnp.bfloat16)
    keys_tok = projected[:, 1].astype(jnp.bfloat16)
    values_tok = (projected[:, 2] + qv_bias[1]).astype(jnp.bfloat16)
    query_win = to_windows(queries.reshape(tokens_here, heads_here, HEAD_DIM), images)
    key_win = to_windows(keys_tok.reshape(tokens_here, heads_here, HEAD_DIM), images)
    value_win = to_windows(values_tok.reshape(tokens_here, heads_here, HEAD_DIM), images)
    region_win = (
        regions.reshape(across, WIN, across, WIN)
        .transpose(0, 2, 1, 3)
        .reshape(across * across, positions)
    )
    allowed = region_win[:, :, None] == region_win[:, None, :]
    one_hot = (
        rel_index.reshape(-1)[:, None] == jnp.arange(bias_table.shape[0], dtype=jnp.int32)[None, :]
    ).astype(jnp.float32)
    rel_bias = jnp.dot(one_hot, bias_table, precision=lax.Precision.HIGHEST).T.reshape(
        heads_here, positions, positions
    )
    scores = window_scores(query_win, key_win, rel_bias, allowed, images)
    top_score = jnp.max(scores, axis=-1, keepdims=True)
    log_total = top_score + jnp.log(jnp.sum(jnp.exp(scores - top_score), axis=-1, keepdims=True))
    prob_b = (
        jnp.exp(scores - log_total)
        .astype(jnp.bfloat16)
        .reshape(-1, heads_here, positions, positions)
    )
    mixed = jnp.einsum("whij,whje->whie", prob_b, value_win, preferred_element_type=jnp.float32)
    mixed_tok = from_windows(mixed.astype(jnp.bfloat16), images)
    attn_part = jnp.dot(mixed_tok, w_proj, preferred_element_type=jnp.float32)
    attn_total = lax.psum(attn_part.astype(jnp.bfloat16), "tensor").astype(jnp.float32)
    hidden_res = residual_in + attn_total + proj_bias
    normed_two, unit_two, inverse_two = layer_norm(hidden_res, ln2_gain, ln2_shift)
    normed_two_b = normed_two.astype(jnp.bfloat16)
    pre_act = jnp.dot(normed_two_b, w_fc1, preferred_element_type=jnp.float32) + fc1_bias
    activ_b = gelu_exact(pre_act).astype(jnp.bfloat16)
    mlp_part = jnp.dot(activ_b, w_fc2, preferred_element_type=jnp.float32)
    mlp_total = lax.psum(mlp_part.astype(jnp.bfloat16), "tensor").astype(jnp.float32)
    output = (hidden_res + mlp_total + fc2_bias).astype(jnp.bfloat16)
    upstream = grad_output.astype(jnp.float32)
    grad_fc2_bias = jnp.sum(upstream, axis=0)
    grad_fc2 = jnp.dot(activ_b.T, grad_output, preferred_element_type=jnp.float32)
    grad_act = jnp.dot(grad_output, w_fc2.T, preferred_element_type=jnp.float32)
    grad_pre = grad_act * gelu_slope(pre_act)
    grad_pre_b = grad_pre.astype(jnp.bfloat16)
    grad_fc1_bias = jnp.sum(grad_pre, axis=0)
    grad_fc1 = jnp.dot(normed_two_b.T, grad_pre_b, preferred_element_type=jnp.float32)
    back_two_part = jnp.dot(grad_pre_b, w_fc1.T, preferred_element_type=jnp.float32)
    back_two = lax.psum(back_two_part.astype(jnp.bfloat16), "tensor").astype(jnp.float32)
    grad_ln2_gain = jnp.sum(back_two * unit_two, axis=0)
    grad_ln2_shift = jnp.sum(back_two, axis=0)
    mlp_sums = (grad_ln2_gain, grad_ln2_shift, grad_fc1, grad_fc1_bias, grad_fc2, grad_fc2_bias)
    grad_hidden = upstream + norm_backward(back_two, unit_two, inverse_two, ln2_gain)
    grad_hidden_b = grad_hidden.astype(jnp.bfloat16)
    grad_proj_bias = jnp.sum(grad_hidden, axis=0)
    grad_proj = jnp.dot(mixed_tok.T, grad_hidden_b, preferred_element_type=jnp.float32)
    grad_mixed = jnp.dot(grad_hidden_b, w_proj.T, preferred_element_type=jnp.float32).astype(
        jnp.bfloat16
    )
    grad_mixed_win = to_windows(grad_mixed.reshape(tokens_here, heads_here, HEAD_DIM), images)
    scores_again = window_scores(query_win, key_win, rel_bias, allowed, images)
    prob_again = jnp.exp(scores_again - log_total)
    prob_again_b = prob_again.astype(jnp.bfloat16).reshape(-1, heads_here, positions, positions)
    grad_prob = jnp.einsum(
        "whie,whje->whij", grad_mixed_win, value_win, preferred_element_type=jnp.float32
    ).reshape(prob_again.shape)
    row_dot = jnp.sum(prob_again * grad_prob, axis=-1, keepdims=True)
    grad_score = prob_again * (grad_prob - row_dot)
    summed_scores = jnp.sum(grad_score, axis=(0, 1)).reshape(heads_here, positions * positions)
    grad_table = jnp.dot(one_hot.T, summed_scores.T, precision=lax.Precision.HIGHEST)
    grad_score_b = grad_score.astype(jnp.bfloat16).reshape(-1, heads_here, positions, positions)
    grad_query_win = (
        jnp.einsum("whij,whje->whie", grad_score_b, key_win, preferred_element_type=jnp.float32)
        * q_factor
    )
    grad_key_win = jnp.einsum(
        "whij,whie->whje", grad_score_b, query_win, preferred_element_type=jnp.float32
    )
    grad_value_win = jnp.einsum(
        "whij,whie->whje", prob_again_b, grad_mixed_win, preferred_element_type=jnp.float32
    )
    grad_query = from_windows(grad_query_win, images)
    grad_key = from_windows(grad_key_win, images)
    grad_value = from_windows(grad_value_win, images)
    grad_qv_bias = jnp.stack([jnp.sum(grad_query, axis=0), jnp.sum(grad_value, axis=0)])
    grad_three = (
        jnp.stack([grad_query, grad_key, grad_value], axis=1)
        .astype(jnp.bfloat16)
        .reshape(tokens_here, 3 * inner)
    )
    grad_qkv = jnp.dot(normed_one_b.T, grad_three, preferred_element_type=jnp.float32).reshape(
        width, 3, inner
    )
    back_one_part = jnp.dot(grad_three, qkv_weight.T, preferred_element_type=jnp.float32)
    back_one = lax.psum(back_one_part.astype(jnp.bfloat16), "tensor").astype(jnp.float32)
    grad_ln1_gain = jnp.sum(back_one * unit_one, axis=0)
    grad_ln1_shift = jnp.sum(back_one, axis=0)
    grad_input = grad_hidden + norm_backward(back_one, unit_one, inverse_one, ln1_gain)
    total_grads = tuple(
        lax.psum(
            (
                grad_ln1_gain,
                grad_ln1_shift,
                grad_qkv,
                grad_qv_bias,
                grad_table,
                grad_proj,
                grad_proj_bias,
                mlp_sums[0],
                mlp_sums[1],
                mlp_sums[2],
                mlp_sums[3],
                mlp_sums[4],
                mlp_sums[5],
            ),
            "dp",
        )
    )
    return (output, grad_input) + total_grads


def solution(mesh):
    return jax.shard_map(
        local,
        mesh=mesh,
        in_specs=(
            P("dp", None),
            P(),
            P(),
            P(None, None, "tensor"),
            P(None, "tensor"),
            P(None, "tensor"),
            P(),
            P(),
            P("tensor", None),
            P(),
            P(),
            P(),
            P(None, "tensor"),
            P("tensor"),
            P("tensor", None),
            P(),
            P("dp", None),
        ),
        out_specs=(
            P("dp", None),
            P("dp", None),
            P(),
            P(),
            P(None, None, "tensor"),
            P(None, "tensor"),
            P(None, "tensor"),
            P("tensor", None),
            P(),
            P(),
            P(),
            P(None, "tensor"),
            P("tensor"),
            P("tensor", None),
            P(),
        ),
        check_vma=False,
    )
```

profile of v0, /device:TPU:0, one launch (start us, length us, event | category | flops | bytes accessed | tf_op | source)
XLA Modules:
  0.0 338.9 jit_solution(2142861799854349741)
XLA Ops:
  7.3 1.2 convert_reduce_fusion.2
  8.5 1.2 fusion.26
  9.8 1.4 copy.96
  14.7 1.4 squeeze.7
  19.8 1.2 convolution_bitcast_fusion
  22.4 1.3 copy.100
  24.2 1.4 copy.99
  25.6 2.0 fusion.72
  29.9 2.4 copy.104
  32.3 2.2 convolution_convert_fusion
  34.5 2.4 copy.105
  37.0 1.2 copy.106
  39.3 1.7 reshape.250
  41.1 2.0 convolution_convert_fusion.3
  43.4 28.6 %all-reduce.8.cloned.1.call-done = bf16[392,512]{1,0:T(8,128)(2,1)} async-done(((bf16[392,512]{1,0:T(8,128)(2,1)}), bf16[392,512]{1,0:T(8,128)(2,1)}) %all-reduce.8.cloned.1.call-update) | async-done | bytes 401424 | tf_op jit(solution)/shard_map/psum | solution.py:139
  72.0 1.3 fusion.55
  73.3 1.3 multiply_reduce_fusion.1
  74.7 1.8 multiply_convert_fusion
  76.5 1.6 fusion.73
  78.9 1.4 convolution_convert_fusion.1
  80.4 2.9 convolution_convert_fusion.2
  83.3 2.2 fusion.52
  85.6 21.0 %all-reduce.10.cloned.1.call-done = bf16[392,512]{1,0:T(8,128)(2,1)} async-done(((bf16[392,512]{1,0:T(8,128)(2,1)}), bf16[392,512]{1,0:T(8,128)(2,1)}) %all-reduce.10.cloned.1.call-update) | async-done | bytes 401424 | tf_op jit(solution)/shard_map/psum | solution.py:157
  106.6 2.2 fusion.32
  108.8 2.3 fusion.65
  111.4 1.2 reshape_reshape.2
  113.6 1.1 slice.178
  116.0 2.4 copy.108
  118.4 2.6 fusion.56
  121.0 3.0 copy.120
  124.1 1.5 copy.121
  126.4 1.1 slice.187
  128.3 1.3 fusion.66
  130.6 1.4 convolution_multiply_fusion
  133.5 1.9 copy.112
  135.7 1.2 copy-done.3
  139.0 1.2 stack_reshape.10
  142.6 2.5 fusion.8
  145.5 2.1 fusion.74
  148.7 1.9 fusion.45
  152.9 27.3 %all-reduce.14.cloned.1.call-done = (bf16[392,512]{1,0:T(8,128)(2,1)}, bf16[392,512]{1,0:T(8,128)(2,1)}) async-done(((bf16[392,512]{1,0:T(8,128)(2,1)}, bf16[392,512]{1,0:T(8,128)(2,1)}), (bf16[392,512]{1,0:T(8,128)(2,1)}, bf16[392,512]{1,0:T(8,128)(2,1)})) %all-reduce.14.cloned.1.call-update) | async-done | bytes 802832 | tf_op jit(solution)/shard_map/psum | solution.py:146
  180.2 1.5 fusion.33
  181.8 63.3 %all-reduce = (f32[512]{0:T(512)}, f32[512]{0:T(512)}, f32[2,256]{1,0:T(2,128)}, f32[169,8]{0,1:T(8,128)}, f32[512]{0:T(512)}, /*index=5*/f32[512]{0:T(512)}, f32[512]{0:T(512)}, f32[1024]{0:T(1024)}, f32[512]{0:T(512)}) all-reduce(f32[512]{0:T(512)S(1)} %get-tuple-element.17, ...), channel_id=1, replica_groups=mesh['dp'=16,'tensor'=2] {'dp'}, use_global_device_ids=true, to_apply=%region_16.17 | all-reduce | flops 5960 | bytes 47680 | tf_op jit(solution)/shard_map/psum | solution.py:208
  245.1 2.6 fusion.25
  247.7 77.4 %all-reduce.12.cloned.1.call-done = (f32[512,3,256]{2,0,1:T(8,128)}, f32[256,512]{1,0:T(8,128)}, f32[512,1024]{1,0:T(8,128)}, f32[1024,512]{1,0:T(8,128)}) async-done(((f32[512,3,256]{2,0,1:T(8,128)}, f32[256,512]{1,0:T(8,128)}, f32[512,1024]{1,0:T(8,128)}, f32[1024,512]{1,0:T(8,128)}), (f32[512,3,256]{2,0,1:T(8,128)}, f32[256,512]{1,0:T(8,128)}, f32[512,1024]{1,0:T(8,128)}, ...) | async-done | bytes 6291472 | tf_op jit(solution)/shard_map/psum | solution.py:208
  325.1 2.8 copy.146
  328.7 1.3 copy.148
  331.0 1.3 copy.149
  (205 shorter events, 30.4 us)
Async XLA Ops:
  7.2 67.4 %copy-start = (bf16[512,1024]{1,0:T(8,128)(2,1)S(1)}, bf16[512,1024]{1,0:T(8,128)(2,1)}, u32[]{:S(2)}) copy-start(bf16[512,1024]{1,0:T(8,128)(2,1)} %param.29) | copy-start | bytes 3145732
  7.2 4.0 %copy-start.2 = (bf16[392,512]{1,0:T(8,128)(2,1)S(1)}, bf16[392,512]{1,0:T(8,128)(2,1)}, u32[]{:S(2)}) copy-start(bf16[392,512]{1,0:T(8,128)(2,1)} %param.17) | copy-start | bytes 1204228
  7.2 4.0 %copy-start.42 = (f32[512]{0:T(512)S(1)}, f32[512]{0:T(512)}, u32[]{:S(2)}) copy-start(f32[512]{0:T(512)} %param.18) | copy-start | bytes 6148
  7.2 4.0 %copy-start.56 = (f32[512]{0:T(512)S(1)}, f32[512]{0:T(512)}, u32[]{:S(2)}) copy-start(f32[512]{0:T(512)} %param.19) | copy-start | bytes 6148
  7.2 64.8 %all-reduce.8.cloned.1.call-start = ((), (), s32[]{:S(2)}) async-start(), calls=%async_computation | async-start | bytes 802816 | tf_op jit(solution)/shard_map/psum | solution.py:139
  9.8 2.0 copy-start.35
  12.7 1.9 copy-start.50
  18.4 3.6 %copy-start.8 = (bf16[2,11,14,8,32]{4,3,2,1,0:T(8,128)(2,1)S(1)}, bf16[2,11,14,8,32]{4,3,2,1,0:T(8,128)(2,1)}, u32[]{:S(2)}) copy-start(bf16[2,11,14,8,32]{4,3,2,1,0:T(8,128)(2,1)} %slice.167) | copy-start | bytes 473092
  18.4 3.6 %copy-start.22 = (bf16[2,3,14,8,32]{4,3,2,1,0:T(8,128)(2,1)S(1)}, bf16[2,3,14,8,32]{4,3,2,1,0:T(8,128)(2,1)}, u32[]{:S(2)}) copy-start(bf16[2,3,14,8,32]{4,3,2,1,0:T(8,128)(2,1)} %slice.168) | copy-start | bytes 129028
  19.4 2.9 copy-start.38
  28.6 3.7 %copy-start.26 = (f32[8,8,49]{2,1,0:T(8,128)}, f32[8,8,49]{2,1,0:T(8,128)S(1)}, u32[]{:S(2)}) copy-start(f32[8,8,49]{2,1,0:T(8,128)S(1)} %log_add_fusion) | copy-start | bytes 37636
  38.2 33.8 %copy-start.32 = (f32[512]{0:T(512)S(1)}, f32[512]{0:T(512)}, u32[]{:S(2)}) copy-start(f32[512]{0:T(512)} %param.26) | copy-start | bytes 6148
  41.0 35.4 %copy-start.18 = (bf16[392,256]{1,0:T(8,128)(2,1)}, bf16[392,256]{1,0:T(8,128)(2,1)S(1)}, u32[]{:S(2)}) copy-start(bf16[392,256]{1,0:T(8,128)(2,1)S(1)} %reshape.250) | copy-start | bytes 602116
  41.1 33.6 %copy-start.40 = (f32[512]{0:T(512)S(1)}, f32[512]{0:T(512)}, u32[]{:S(2)}) copy-start(f32[512]{0:T(512)} %param.27) | copy-start | bytes 6148
  41.1 33.6 %copy-start.54 = (f32[1024]{0:T(1024)S(1)}, f32[1024]{0:T(1024)}, u32[]{:S(2)}) copy-start(f32[1024]{0:T(1024)} %param.30) | copy-start | bytes 12292
  41.1 33.6 %copy-start.55 = (f32[512]{0:T(512)S(1)}, f32[512]{0:T(512)}, u32[]{:S(2)}) copy-start(f32[512]{0:T(512)} %param.28) | copy-start | bytes 6148
  43.2 63.4 %all-reduce.10.cloned.1.call-start = ((), (), s32[]{:S(2)}) async-start(), calls=%async_computation.1 | async-start | bytes 802816 | tf_op jit(solution)/shard_map/psum | solution.py:157
  72.0 2.6 copy-start.4
  73.3 10.0 %copy-start.33 = (f32[392]{0:T(512)}, f32[392]{0:T(512)S(1)}, u32[]{:S(2)}) copy-start(f32[392]{0:T(512)S(1)} %broadcast_multiply_fusion.4) | copy-start | bytes 4708
  74.7 8.6 %copy-start.37 = (f32[392]{0:T(512)}, f32[392]{0:T(512)S(1)}, u32[]{:S(2)}) copy-start(f32[392]{0:T(512)S(1)} %add_rsqrt_fusion) | copy-start | bytes 4708
  74.7 1.8 copy-start.20
  80.3 3.0 copy-start.5
  80.3 99.9 %all-reduce.14.cloned.1.call-start = ((), (), s32[]{:S(2)}) async-start(), calls=%async_computation.3 | async-start | bytes 1605632 | tf_op jit(solution)/shard_map/psum | solution.py:146
  80.4 2.9 copy-start.59
  83.3 23.3 %copy-start.41 = (f32[512]{0:T(512)S(1)}, f32[512]{0:T(512)}, u32[]{:S(2)}) copy-start(f32[512]{0:T(512)} %param.27) | copy-start | bytes 6148
  85.6 25.5 %copy-start.24 = (bf16[256,512]{1,0:T(8,128)(2,1)S(1)}, bf16[256,512]{1,0:T(8,128)(2,1)}, u32[]{:S(2)}) copy-start(bf16[256,512]{1,0:T(8,128)(2,1)} %param.25) | copy-start | bytes 786436
  115.0 3.4 %copy-start.27 = (f32[8,8,49]{2,1,0:T(8,128)S(1)}, f32[8,8,49]{2,1,0:T(8,128)}, u32[]{:S(2)}) copy-start(f32[8,8,49]{2,1,0:T(8,128)} %copy-done.26) | copy-start | bytes 37636
  125.6 1.9 copy-start.12
  125.6 1.9 copy-start.13
  139.0 2.9 copy-start.29
  142.6 2.9 copy-start.21
  142.6 2.9 copy-start.28
  145.2 2.4 copy-start.19
  145.2 3.5 %copy-start.36 = (f32[392]{0:T(512)S(1)}, f32[392]{0:T(512)}, u32[]{:S(2)}) copy-start(f32[392]{0:T(512)} %copy-done.35) | copy-start | bytes 4708
  145.2 3.5 %copy-start.43 = (f32[512]{0:T(512)S(1)}, f32[512]{0:T(512)}, u32[]{:S(2)}) copy-start(f32[512]{0:T(512)} %param.18) | copy-start | bytes 6148
  145.2 3.5 %copy-start.57 = (f32[512]{0:T(512)S(1)}, f32[512]{0:T(512)}, u32[]{:S(2)}) copy-start(f32[512]{0:T(512)} %param.19) | copy-start | bytes 6148
  145.2 179.9 %all-reduce.12.cloned.1.call-start = ((), (), s32[]{:S(2)}) async-start(), calls=%async_computation.2 | async-start | bytes 12582912 | tf_op jit(solution)/shard_map/psum | solution.py:208
  150.7 31.1 %copy-start.44 = (f32[512]{0:T(512)S(1)}, f32[512]{0:T(512)}, u32[]{:S(2)}) copy-start(f32[512]{0:T(512)} %get-tuple-element.15) | copy-start | bytes 6148
  150.7 31.1 %copy-start.45 = (f32[512]{0:T(512)S(1)}, f32[512]{0:T(512)}, u32[]{:S(2)}) copy-start(f32[512]{0:T(512)} %get-tuple-element.21) | copy-start | bytes 6148
  150.7 31.1 %copy-start.46 = (f32[512]{0:T(512)S(1)}, f32[512]{0:T(512)}, u32[]{:S(2)}) copy-start(f32[512]{0:T(512)} %get-tuple-element.40) | copy-start | bytes 6148
  150.7 31.1 %copy-start.47 = (f32[512]{0:T(512)S(1)}, f32[512]{0:T(512)}, u32[]{:S(2)}) copy-start(f32[512]{0:T(512)} %get-tuple-element.54) | copy-start | bytes 6148
  150.7 31.1 %copy-start.48 = (f32[1024]{0:T(1024)S(1)}, f32[1024]{0:T(1024)}, u32[]{:S(2)}) copy-start(f32[1024]{0:T(1024)} %get-tuple-element.63) | copy-start | bytes 12292
  150.7 94.4 %copy-start.6 = (bf16[392,512]{1,0:T(8,128)(2,1)S(1)}, bf16[392,512]{1,0:T(8,128)(2,1)}, u32[]{:S(2)}) copy-start(bf16[392,512]{1,0:T(8,128)(2,1)} %all-reduce.8.cloned.1.call-done) | copy-start | bytes 1204228
  150.7 94.4 %copy-start.49 = (f32[512]{0:T(512)S(1)}, f32[512]{0:T(512)}, u32[]{:S(2)}) copy-start(f32[512]{0:T(512)} %param.32) | copy-start | bytes 6148
  325.1 2.8 copy-start.30
  325.1 3.6 %copy-start.17 = (f32[512,1024]{1,0:T(8,128)S(1)}, f32[512,1024]{1,0:T(8,128)}, u32[]{:S(2)}) copy-start(f32[512,1024]{1,0:T(8,128)} %get-tuple-element.92) | copy-start | bytes 6291460
  328.7 2.3 copy-start.16
  328.7 3.7 %copy-start.1 = (bf16[512,1024]{1,0:T(8,128)(2,1)S(1)}, bf16[512,1024]{1,0:T(8,128)(2,1)}, u32[]{:S(2)}) copy-start(bf16[512,1024]{1,0:T(8,128)(2,1)} %param.29) | copy-start | bytes 3145732
  (16 other events, 20.1 us)
Sparse Core Ops, SparseCore 0:
  43.3 28.6 all-reduce.7
  80.5 26.1 all-reduce.9
  145.3 34.8 all-reduce.13
  185.2 139.8 all-reduce.11
where the time goes:
time: 340 us; the launch traced here: 339 us
  waiting for transfers between devices  154 us (45%)
  blocking collectives  63.3 us (19%)
  local copies, waits for them, and re-layouts  53.2 us (16%)
  matrix products  32 us (9%)
  other arithmetic  20.7 us (6%)
  between operations  14.7 us (4%)
    psum x1, waiting for transfers between devices, local(): lax.psum((grad_ln1_gain, grad_ln1_shift, grad_qkv, grad_qv_bias, grad_tab...  77.4 us
    psum x1, blocking collectives, local(): lax.psum((grad_ln1_gain, grad_ln1_shift, grad_qkv, grad_qv_bias, grad_tab...  63.3 us
    psum x1, waiting for transfers between devices, local(): lax.psum(attn_part.astype(jnp.bfloat16), 'tensor').astype(jnp.float32)  28.6 us
    psum x1, waiting for transfers between devices, local(): lax.psum(mlp_part.astype(jnp.bfloat16), 'tensor').astype(jnp.float32)  27.3 us
    psum x1, waiting for transfers between devices, local(): lax.psum(back_two_part.astype(jnp.bfloat16), 'tensor').astype(jnp.float32)  21 us
    unnamed x125, local copies, waits for them, and re-layouts  13.7 us
    reshape x4, local copies, waits for them, and re-layouts, to_windows(): layout.reshape(images * across * across, heads_here, WIN * WIN, head_depth)  7.54 us
  transfers between devices with their start and end apart: 4, of which 4 were waited for; matrix products, arithmetic and copies ran while one was open for 5% of the time, Pallas kernels for 0%

commit v1 on v0

--- a/solution.py
+++ b/solution.py
@@ -136,7 +136,9 @@
     mixed = jnp.einsum("whij,whje->whie", prob_b, value_win, preferred_element_type=jnp.float32)
     mixed_tok = from_windows(mixed.astype(jnp.bfloat16), images)
     attn_part = jnp.dot(mixed_tok, w_proj, preferred_element_type=jnp.float32)
-    attn_total = lax.psum(attn_part.astype(jnp.bfloat16), "tensor").astype(jnp.float32)
+    attn_total = jnp.sum(lax.all_gather(attn_part.astype(jnp.bfloat16), "tensor"), axis=0).astype(
+        jnp.float32
+    )
     hidden_res = residual_in + attn_total + proj_bias
     normed_two, unit_two, inverse_two = layer_norm(hidden_res, ln2_gain, ln2_shift)
     normed_two_b = normed_two.astype(jnp.bfloat16)

time: 340 us -> 324 us (0.953)
  waiting for transfers between devices: 154 us -> 127 us
  blocking collectives: 63.3 us -> 76.5 us
    psum x1 -> x0, waiting for transfers between devices: 28.6 us -> none  [local(): lax.psum(attn_part.astype(jnp.bfloat16), 'tensor').astype(jnp.float32)]
    all_gather x0 -> x1, blocking collectives: none -> 13.2 us  [local(): lax.all_gather(attn_part.astype(jnp.bfloat16), 'tensor')]
    unnamed x125 -> x129, local copies, waits for them, and re-layouts: 13.7 us -> 14.6 us
  transfers between devices with their start and end apart: 4 -> 3, of which waited for: 4 -> 3; matrix products, arithmetic and copies ran while one was open for 5% -> 5% of each run, Pallas kernels for 0% -> 0%
where the time goes in v1:
time: 324 us; the launch traced here: 323 us
  waiting for transfers between devices  127 us (39%)
  blocking collectives  76.5 us (24%)
  local copies, waits for them, and re-layouts  53.3 us (16%)
  matrix products  30.2 us (9%)
  other arithmetic  20.6 us (6%)
  between operations  14.7 us (5%)
    psum x1, waiting for transfers between devices, local(): lax.psum((grad_ln1_gain, grad_ln1_shift, grad_qkv, grad_qv_bias, grad_tab...  77.6 us
    psum x1, blocking collectives, local(): lax.psum((grad_ln1_gain, grad_ln1_shift, grad_qkv, grad_qv_bias, grad_tab...  63.3 us
    psum x1, waiting for transfers between devices, local(): lax.psum(mlp_part.astype(jnp.bfloat16), 'tensor').astype(jnp.float32)  27.2 us
    psum x1, waiting for transfers between devices, local(): lax.psum(back_two_part.astype(jnp.bfloat16), 'tensor').astype(jnp.float32)  22.4 us
    unnamed x129, local copies, waits for them, and re-layouts  14.6 us
    all_gather x1, blocking collectives, local(): lax.all_gather(attn_part.astype(jnp.bfloat16), 'tensor')  13.2 us
    reshape x4, local copies, waits for them, and re-layouts, to_windows(): layout.reshape(images * across * across, heads_here, WIN * WIN, head_depth)  6.79 us
  transfers between devices with their start and end apart: 3, of which 3 were waited for; matrix products, arithmetic and copies ran while one was open for 5% of the time, Pallas kernels for 0%

profile of v1, /device:TPU:0, one launch (start us, length us, event | category | flops | bytes accessed | tf_op | source)
XLA Modules:
  0.0 322.9 jit_solution(7107853855783026210)
XLA Ops:
  7.3 1.2 convert_reduce_fusion.2
  8.5 1.2 fusion.26
  9.8 1.4 copy.96
  14.7 1.4 squeeze.7
  19.8 1.2 convolution_bitcast_fusion
  22.4 1.3 copy.100
  24.2 1.4 copy.99
  25.6 2.0 fusion.72
  29.9 2.4 copy.104
  32.3 2.2 convolution_convert_fusion
  34.6 2.4 copy.105
  37.0 1.2 copy.106
  39.3 1.7 reshape.250
  41.1 1.3 convolution_convert_fusion.3
  42.4 13.2 %all-gather = bf16[784,512]{1,0:T(8,128)(2,1)} all-gather(bf16[392,512]{1,0:T(8,128)(2,1)S(1)} %convolution_convert_fusion.3), channel_id=2, replica_groups=mesh['dp'=16,'tensor'=2] {'tensor'}, dimensions={0}, use_global_device_ids=true | all-gather | bytes 1204224 | tf_op jit(solution)/shard_map/all_gather | solution.py:139
  55.6 2.1 reduce_sum.227
  57.8 1.3 fusion.55
  59.1 1.3 multiply_reduce_fusion.1
  60.4 1.8 multiply_convert_fusion
  62.2 1.6 fusion.73
  64.7 1.4 convolution_convert_fusion.1
  66.1 2.9 convolution_convert_fusion.2
  69.1 2.2 fusion.52
  71.3 22.4 %all-reduce.7.cloned.1.call-done = bf16[392,512]{1,0:T(8,128)(2,1)} async-done(((bf16[392,512]{1,0:T(8,128)(2,1)}), bf16[392,512]{1,0:T(8,128)(2,1)}) %all-reduce.7.cloned.1.call-update) | async-done | bytes 401424 | tf_op jit(solution)/shard_map/psum | solution.py:159
  93.7 1.6 fusion.32
  95.3 1.5 fusion.65
  98.0 1.2 reshape_reshape.2
  100.2 1.1 slice.178
  102.6 1.6 copy.108
  104.2 1.6 fusion.56
  105.8 3.0 copy.120
  108.8 1.5 copy.121
  113.0 1.3 fusion.66
  115.4 1.4 convolution_multiply_fusion
  118.3 1.9 copy.112
  120.5 1.2 copy-done.7
  123.8 1.2 stack_reshape.10
  126.5 2.5 fusion.8
  129.4 2.1 fusion.74
  132.6 1.9 fusion.45
  136.9 27.2 %all-reduce.11.cloned.1.call-done = (bf16[392,512]{1,0:T(8,128)(2,1)}, bf16[392,512]{1,0:T(8,128)(2,1)}) async-done(((bf16[392,512]{1,0:T(8,128)(2,1)}, bf16[392,512]{1,0:T(8,128)(2,1)}), (bf16[392,512]{1,0:T(8,128)(2,1)}, bf16[392,512]{1,0:T(8,128)(2,1)})) %all-reduce.11.cloned.1.call-update) | async-done | bytes 802832 | tf_op jit(solution)/shard_map/psum | solution.py:148
  164.1 1.5 fusion.33
  165.6 63.3 %all-reduce = (f32[512]{0:T(512)}, f32[512]{0:T(512)}, f32[2,256]{1,0:T(2,128)}, f32[169,8]{0,1:T(8,128)}, f32[512]{0:T(512)}, /*index=5*/f32[512]{0:T(512)}, f32[512]{0:T(512)}, f32[1024]{0:T(1024)}, f32[512]{0:T(512)}) all-reduce(f32[512]{0:T(512)S(1)} %get-tuple-element.17, ...), channel_id=1, replica_groups=mesh['dp'=16,'tensor'=2] {'dp'}, use_global_device_ids=true, to_apply=%region_16.17 | all-reduce | flops 5960 | bytes 47680 | tf_op jit(solution)/shard_map/psum | solution.py:210
  228.9 2.6 fusion.25
  231.5 77.6 %all-reduce.9.cloned.1.call-done = (f32[512,3,256]{2,0,1:T(8,128)}, f32[256,512]{1,0:T(8,128)}, f32[512,1024]{1,0:T(8,128)}, f32[1024,512]{1,0:T(8,128)}) async-done(((f32[512,3,256]{2,0,1:T(8,128)}, f32[256,512]{1,0:T(8,128)}, f32[512,1024]{1,0:T(8,128)}, f32[1024,512]{1,0:T(8,128)}), (f32[512,3,256]{2,0,1:T(8,128)}, f32[256,512]{1,0:T(8,128)}, f32[512,1024]{1,0:T(8,128)}, ...) | async-done | bytes 6291472 | tf_op jit(solution)/shard_map/psum | solution.py:210
  309.1 2.8 copy.145
  312.7 1.3 copy.147
  315.0 1.3 copy.148
  (208 shorter events, 31.3 us)
Async XLA Ops:
  7.2 53.2 %copy-start = (bf16[512,1024]{1,0:T(8,128)(2,1)S(1)}, bf16[512,1024]{1,0:T(8,128)(2,1)}, u32[]{:S(2)}) copy-start(bf16[512,1024]{1,0:T(8,128)(2,1)} %param.29) | copy-start | bytes 3145732
  7.2 4.0 %copy-start.2 = (bf16[392,512]{1,0:T(8,128)(2,1)S(1)}, bf16[392,512]{1,0:T(8,128)(2,1)}, u32[]{:S(2)}) copy-start(bf16[392,512]{1,0:T(8,128)(2,1)} %param.17) | copy-start | bytes 1204228
  7.2 4.0 %copy-start.48 = (f32[512]{0:T(512)S(1)}, f32[512]{0:T(512)}, u32[]{:S(2)}) copy-start(f32[512]{0:T(512)} %param.18) | copy-start | bytes 6148
  7.2 4.0 %copy-start.58 = (f32[512]{0:T(512)S(1)}, f32[512]{0:T(512)}, u32[]{:S(2)}) copy-start(f32[512]{0:T(512)} %param.19) | copy-start | bytes 6148
  7.2 86.5 %all-reduce.7.cloned.1.call-start = ((), (), s32[]{:S(2)}) async-start(), calls=%async_computation | async-start | bytes 802816 | tf_op jit(solution)/shard_map/psum | solution.py:159
  9.8 2.0 copy-start.41
  12.7 1.9 copy-start.52
  18.4 3.6 %copy-start.9 = (bf16[2,11,14,8,32]{4,3,2,1,0:T(8,128)(2,1)S(1)}, bf16[2,11,14,8,32]{4,3,2,1,0:T(8,128)(2,1)}, u32[]{:S(2)}) copy-start(bf16[2,11,14,8,32]{4,3,2,1,0:T(8,128)(2,1)} %slice.167) | copy-start | bytes 473092
  18.4 3.6 %copy-start.25 = (bf16[2,3,14,8,32]{4,3,2,1,0:T(8,128)(2,1)S(1)}, bf16[2,3,14,8,32]{4,3,2,1,0:T(8,128)(2,1)}, u32[]{:S(2)}) copy-start(bf16[2,3,14,8,32]{4,3,2,1,0:T(8,128)(2,1)} %slice.168) | copy-start | bytes 129028
  19.4 2.9 copy-start.44
  28.6 3.7 %copy-start.29 = (f32[8,8,49]{2,1,0:T(8,128)}, f32[8,8,49]{2,1,0:T(8,128)S(1)}, u32[]{:S(2)}) copy-start(f32[8,8,49]{2,1,0:T(8,128)S(1)} %log_add_fusion) | copy-start | bytes 37636
  41.1 16.7 %copy-start.20 = (bf16[392,256]{1,0:T(8,128)(2,1)}, bf16[392,256]{1,0:T(8,128)(2,1)S(1)}, u32[]{:S(2)}) copy-start(bf16[392,256]{1,0:T(8,128)(2,1)S(1)} %reshape.250) | copy-start | bytes 602116
  41.1 16.7 %copy-start.38 = (f32[512]{0:T(512)S(1)}, f32[512]{0:T(512)}, u32[]{:S(2)}) copy-start(f32[512]{0:T(512)} %param.26) | copy-start | bytes 6148
  55.6 4.8 %copy-start.46 = (f32[512]{0:T(512)S(1)}, f32[512]{0:T(512)}, u32[]{:S(2)}) copy-start(f32[512]{0:T(512)} %param.27) | copy-start | bytes 6148
  55.6 4.8 %copy-start.56 = (f32[1024]{0:T(1024)S(1)}, f32[1024]{0:T(1024)}, u32[]{:S(2)}) copy-start(f32[1024]{0:T(1024)} %param.30) | copy-start | bytes 12292
  55.6 4.8 %copy-start.57 = (f32[512]{0:T(512)S(1)}, f32[512]{0:T(512)}, u32[]{:S(2)}) copy-start(f32[512]{0:T(512)} %param.28) | copy-start | bytes 6148
  57.8 2.6 copy-start.3
  59.1 10.0 %copy-start.39 = (f32[392]{0:T(512)}, f32[392]{0:T(512)S(1)}, u32[]{:S(2)}) copy-start(f32[392]{0:T(512)S(1)} %broadcast_multiply_fusion.4) | copy-start | bytes 4708
  60.4 8.6 %copy-start.43 = (f32[392]{0:T(512)}, f32[392]{0:T(512)S(1)}, u32[]{:S(2)}) copy-start(f32[392]{0:T(512)S(1)} %add_rsqrt_fusion) | copy-start | bytes 4708
  60.4 1.8 copy-start.22
  60.4 1.8 copy-start.54
  66.1 3.0 copy-start.4
  66.1 98.0 %all-reduce.11.cloned.1.call-start = ((), (), s32[]{:S(2)}) async-start(), calls=%async_computation.2 | async-start | bytes 1605632 | tf_op jit(solution)/shard_map/psum | solution.py:148
  66.1 2.9 copy-start.61
  69.1 24.6 %copy-start.47 = (f32[512]{0:T(512)S(1)}, f32[512]{0:T(512)}, u32[]{:S(2)}) copy-start(f32[512]{0:T(512)} %param.27) | copy-start | bytes 6148
  69.1 26.2 %copy-start.23 = (bf16[392,512]{1,0:T(8,128)(2,1)S(1)}, bf16[392,512]{1,0:T(8,128)(2,1)}, u32[]{:S(2)}) copy-start(bf16[392,512]{1,0:T(8,128)(2,1)} %param.33) | copy-start | bytes 1204228
  71.3 26.4 %copy-start.27 = (bf16[256,512]{1,0:T(8,128)(2,1)S(1)}, bf16[256,512]{1,0:T(8,128)(2,1)}, u32[]{:S(2)}) copy-start(bf16[256,512]{1,0:T(8,128)(2,1)} %param.25) | copy-start | bytes 786436
  101.6 2.6 copy-start.30
  104.2 1.6 copy-start.14
  110.4 1.9 copy-start.13
  110.4 1.9 copy-start.15
  123.8 1.9 copy-start.32
  126.5 2.5 copy-start.36
  126.5 2.9 copy-start.24
  126.5 2.9 copy-start.31
  129.0 2.5 copy-start.6
  129.0 2.5 copy-start.21
  129.0 3.6 %copy-start.42 = (f32[392]{0:T(512)S(1)}, f32[392]{0:T(512)}, u32[]{:S(2)}) copy-start(f32[392]{0:T(512)} %copy-done.41) | copy-start | bytes 4708
  129.1 3.6 %copy-start.49 = (f32[512]{0:T(512)S(1)}, f32[512]{0:T(512)}, u32[]{:S(2)}) copy-start(f32[512]{0:T(512)} %param.18) | copy-start | bytes 6148
  129.1 3.6 %copy-start.59 = (f32[512]{0:T(512)S(1)}, f32[512]{0:T(512)}, u32[]{:S(2)}) copy-start(f32[512]{0:T(512)} %param.19) | copy-start | bytes 6148
  129.1 180.0 %all-reduce.9.cloned.1.call-start = ((), (), s32[]{:S(2)}) async-start(), calls=%async_computation.1 | async-start | bytes 12582912 | tf_op jit(solution)/shard_map/psum | solution.py:210
  129.4 3.3 %copy-start.37 = (bf16[392,1,256]{2,0,1:T(8,128)(2,1)S(1)}, bf16[392,1,256]{2,0,1:T(8,128)(2,1)}, u32[]{:S(2)}) copy-start(bf16[392,1,256]{2,0,1:T(8,128)(2,1)} %copy-done.36) | copy-start | bytes 602116
  134.6 31.0 %copy-start.50 = (f32[1024]{0:T(1024)S(1)}, f32[1024]{0:T(1024)}, u32[]{:S(2)}) copy-start(f32[1024]{0:T(1024)} %get-tuple-element.63) | copy-start | bytes 12292
  134.6 94.3 %copy-start.51 = (f32[512]{0:T(512)S(1)}, f32[512]{0:T(512)}, u32[]{:S(2)}) copy-start(f32[512]{0:T(512)} %param.32) | copy-start | bytes 6148
  309.1 2.8 copy-start.34
  309.1 3.6 %copy-start.19 = (f32[512,1024]{1,0:T(8,128)S(1)}, f32[512,1024]{1,0:T(8,128)}, u32[]{:S(2)}) copy-start(f32[512,1024]{1,0:T(8,128)} %get-tuple-element.92) | copy-start | bytes 6291460
  312.7 2.3 copy-start.18
  312.7 3.7 %copy-start.1 = (bf16[512,1024]{1,0:T(8,128)(2,1)S(1)}, bf16[512,1024]{1,0:T(8,128)(2,1)}, u32[]{:S(2)}) copy-start(bf16[512,1024]{1,0:T(8,128)(2,1)} %param.29) | copy-start | bytes 3145732
  (17 other events, 20.7 us)
Sparse Core Ops, SparseCore 0:
  66.2 27.4 all-reduce.6
  129.1 34.8 all-reduce.10
  169.2 139.8 all-reduce.8
